TPU v7x, 32 devices: a whole 2x2x4 slice. The times are simulated.
32 devices in a mesh: feed: 8 (over y, x, core), tm: 4 (over z).
Axes of the slice: x: 2, y: 2, z: 4, core: 2. Of those that a mesh axis runs over, the one named last changes fastest.
Arguments:
- voltages: bfloat16 [256, 1048576], P('feed', 'tm'), may hold values from -12 to 12
- filter_taps: float32 [4, 1024], replicated, may hold values from -1 to 1
- delays: float32 [256], P('feed'), may hold values from -64 to 64
- channel_flags: int32 [512], P('feed'), may hold values from 0 to 1, as said below
Outputs:
- visibilities: float32 [512, 256, 256], P(('feed', 'tm'))
Inputs may be any that keep to these rules, and one draw needn't show every extreme that they name: `channel_flags`: channel c belongs to owner c // 64; every owner keeps between 16 and 64 of its channels, and in every draw some owner keeps all of them.
All inputs are finite; a program needn't handle non-finite values.
Results may differ from a plain program's by a relative error of at most 0.0011.
Values may be sent and summed in bfloat16 or wider, within the bound.
A program may use at most 192 MiB of HBM per device.

v0:
```python
import math
import jax
import jax.numpy as jnp
from jax import lax
from jax.sharding import PartitionSpec as P


def passed_along(block, axis, distance):
    devices = range(lax.axis_size(axis))
    route = [(i - distance, i) for i in devices if i - distance in devices]
    return lax.ppermute(block, axis, route)


def build_table(fft_length):
    channels = jnp.arange(fft_length // 2, dtype=jnp.int32)
    samples = jnp.arange(fft_length, dtype=jnp.int32)
    product = channels[:, None] * samples[None, :] % fft_length
    angles = product.astype(jnp.float32) * (2.0 * math.pi / fft_length)
    return jnp.stack([jnp.cos(angles), -jnp.sin(angles)], axis=1).astype(jnp.bfloat16)


def rotate_phase(real_part, imag_part, channels, delay_values, fft_length):
    angles = 2.0 * math.pi / fft_length * channels * delay_values
    cosine = jnp.cos(angles)
    sine_part = jnp.sin(angles)
    factor = 1.0 / math.sqrt(fft_length)
    return (
        (real_part * cosine + imag_part * sine_part) * factor,
        (imag_part * cosine - real_part * sine_part) * factor,
    )


def gram_blocks(turned, local_frame_count, frame_total):
    count_here, inputs_all, columns = turned.shape
    split = turned.reshape(
        count_here, inputs_all, columns // (2 * local_frame_count), 2, local_frame_count
    )
    real_half = split[:, :, :, 0].reshape(count_here, inputs_all, columns // 2)
    imag_half = split[:, :, :, 1].reshape(count_here, inputs_all, columns // 2)
    block_rows = min(128, inputs_all)
    column_index = jnp.arange(inputs_all)[None, :]
    row_blocks = []
    for first in range(0, inputs_all, block_rows):
        last = first + block_rows
        upper = jnp.einsum(
            "cik,cjk->cij",
            turned[:, first:last],
            turned[:, first:],
            preferred_element_type=jnp.float32,
        )
        lower = jnp.einsum(
            "cik,cjk->cij",
            imag_half[:, first:last],
            real_half[:, :last],
            preferred_element_type=jnp.float32,
        )
        lower = lower - jnp.einsum(
            "cik,cjk->cij",
            real_half[:, first:last],
            imag_half[:, :last],
            preferred_element_type=jnp.float32,
        )
        upper_full = jnp.pad(upper, ((0, 0), (0, 0), (first, 0)))
        lower_full = jnp.pad(lower, ((0, 0), (0, 0), (0, inputs_all - last)))
        row_index = jnp.arange(first, last)[:, None]
        row_blocks.append(jnp.where(row_index <= column_index, upper_full, lower_full))
    return jnp.concatenate(row_blocks, axis=1) / frame_total


def on_device(voltages, filter_taps, delays, channel_flags):
    inputs_here, sample_count = voltages.shape
    tap_count, fft_length = filter_taps.shape
    local_frame_count = sample_count // fft_length
    frames = voltages.reshape(inputs_here, local_frame_count, fft_length)
    history = passed_along(frames[:, local_frame_count - (tap_count - 1) :, :], "tm", 1)
    extended = jnp.concatenate([history, frames], axis=1).astype(jnp.float32)
    filtered = filter_taps[0] * extended[:, tap_count - 1 : tap_count - 1 + local_frame_count]
    for tap_index in range(1, tap_count):
        offset = tap_count - 1 - tap_index
        filtered = (
            filtered + filter_taps[tap_index] * extended[:, offset : offset + local_frame_count]
        )
    filtered = filtered.astype(jnp.bfloat16)
    dft_table = build_table(fft_length)
    raw_spectra = jnp.einsum(
        "cpn,isn->cips", dft_table, filtered, preferred_element_type=jnp.float32
    )
    channels = jnp.arange(fft_length // 2).astype(jnp.float32)[:, None, None]
    real_part, imag_part = rotate_phase(
        raw_spectra[:, :, 0], raw_spectra[:, :, 1], channels, delays[None, :, None], fft_length
    )
    spectra = jnp.concatenate([real_part, imag_part], axis=2).astype(jnp.bfloat16)
    time_devices = lax.axis_size("tm")
    frame_total = local_frame_count * time_devices
    channels_here = channel_flags.shape[0] // time_devices
    local_flags = lax.dynamic_slice_in_dim(
        channel_flags, lax.axis_index("tm") * channels_here, channels_here, 0
    )
    turned = lax.all_to_all(spectra, "feed", split_axis=0, concat_axis=1, tiled=True)
    visibility = lax.psum_scatter(
        gram_blocks(turned, local_frame_count, frame_total), "tm", scatter_dimension=0, tiled=True
    )
    return visibility * local_flags[:, None, None].astype(jnp.float32)


def solution(mesh):
    in_specs = (P("feed", "tm"), P(), P("feed"), P("feed"))
    out_specs = P(("feed", "tm"), None, None)
    return jax.shard_map(
        on_device, mesh=mesh, in_specs=in_specs, out_specs=out_specs, check_vma=False
    )
```

profile of v0, /device:TPU:0, one launch (start us, length us, event | category | flops | bytes accessed | tf_op | source)
XLA Modules:
  0.0 797.1 jit_solution(467650899731393742)
XLA Ops:
  6.5 15.4 %copy.23 = bf16[4,8,256,1024]{3,2,1,0:T(8,128)(2,1)S(1)} copy(bf16[4,8,256,1024]{3,1,2,0:T(8,128)(2,1)} %bitcast.67) | data formatting | bytes 33554432
  21.9 0.1 slice.79
  22.1 4.9 collective-permute-start
  27.0 8.5 %negate_convert_fusion = (bf16[512,1,1024]{2,0,1:T(8,128)(2,1)S(1)}, bf16[512,1,1024]{2,0,1:T(8,128)(2,1)S(1)}) fusion(), kind=kLoop, calls=%fused_computation.49 | loop fusion | flops 8912896 | bytes 2097152 | tf_op jit(solution)/shard_map/convert.3
  35.6 0.3 multiply_cosine_fusion
  35.9 12.0 %maximum_convert_fusion = f32[32,259,1024]{2,1,0:T(8,128)} fusion(bf16[32,256,1024]{2,1,0:T(8,128)(2,1)S(1)} %bitcast.66, bf16[32,3,1024]{2,1,0:T(4,128)(2,1)S(1)} %collective-permute-done), kind=kLoop, calls=%fused_computation.8 | loop fusion | flops 33947648 | bytes 50921472 | tf_op jit(solution)/shard_map/convert_element_type | solution.py:76
  47.9 56.9 %fusion.10 = f32[512,32,2,256]{0,3,2,1:T(8,128)} fusion(f32[32,259,1024]{2,1,0:T(8,128)} %maximum_convert_fusion, f32[1024]{0:T(1024)S(1)} %bitcast.70, f32[1024]{0:T(1024)S(1)} %bitcast.71, f32[1024]{0:T(1024)S(1)} %bitcast.69, f32[1024]{0:T(1024)S(1)} %bitcast.68, bf16[512,1,1024]{2,0,1:T(8,128)(2,1)S(1)} %get-tuple-element.15, ...), kind=kOutput, calls=%fused_computation.20 | convolution fusion | flops 17251172352 | bytes 169885696 | tf_op jit(solution)/shard_map/cpn,isn->cips/dot_general | solution.py:85
  104.8 12.3 %multiply_convert_fusion.1 = (bf16[512,32,256]{0,2,1:T(8,128)(2,1)S(1)}, bf16[512,32,256]{0,2,1:T(8,128)(2,1)S(1)}) fusion(f32[512,32,2,256]{0,3,2,1:T(8,128)} %fusion.10, f32[512,32]{0,1:T(8,128)S(1)} %get-tuple-element.14, f32[512,32]{0,1:T(8,128)S(1)} %get-tuple-element.13), kind=kLoop, calls=%fused_computation.16 | loop fusion | flops 41943040 | bytes 50462720 | tf_op jit(solution)/shard_map/convert
  117.1 6.5 pad_maximum_fusion
  123.6 28.6 %copy.14 = bf16[512,32,512]{2,1,0:T(8,128)(2,1)} copy(bf16[512,32,512]{0,2,1:T(8,128)(2,1)} %pad_maximum_fusion) | data formatting | bytes 33554432 | tf_op jit(solution)/shard_map/concatenate | solution.py:92
  152.3 5.7 all-to-all-start
  158.0 0.2 reduce-scatter.2.cloned.1.call-start
  158.3 0.1 iota_compare_fusion
  158.4 183.6 %all-to-all-done = bf16[512,32,512]{2,1,0:T(8,128)(2,1)} async-done(((bf16[512,32,512]{2,1,0:T(8,128)(2,1)}), bf16[512,32,512]{2,1,0:T(8,128)(2,1)}, u32[]{:S(2)}, u32[]{:S(2)}) %all-to-all-start) | async-done | bytes 16777248 | tf_op jit(solution)/shard_map/all_to_all | solution.py:99
  341.9 14.1 %copy.15 = bf16[64,8,32,512]{3,2,1,0:T(8,128)(2,1)} copy(bf16[64,8,32,512]{3,2,0,1:T(8,128)(2,1)} %bitcast.11) | data formatting | bytes 33554432 | tf_op jit(solution)/shard_map/all_to_all | solution.py:99
  356.0 23.7 %reshape.151 = bf16[64,256,1,2,256]{4,3,1,0,2:T(2,128)(2,1)} reshape(bf16[64,8,32,512]{3,2,1,0:T(8,128)(2,1)} %copy.15) | data formatting | bytes 33554432 | tf_op jit(solution)/shard_map/reshape | solution.py:35
  379.7 32.4 %fusion.45 = (bf16[64,256,1,1,256]{4,3,1,0,2:T(2,128)(2,1)}, bf16[64,256,1,1,256]{4,3,1,0,2:T(2,128)(2,1)}) fusion(bf16[64,256,1,2,256]{4,3,1,0,2:T(2,128)(2,1)} %reshape.151), kind=kLoop, calls=%fused_computation.63 | loop fusion | bytes 33554432 | tf_op jit(solution)/shard_map/slice | solution.py:38
  412.2 8.9 %copy.26 = bf16[64,256,1,1,256]{4,1,0,3,2:T(8,128)(2,1)S(1)} copy(bf16[64,256,1,1,256]{4,3,1,0,2:T(2,128)(2,1)} %get-tuple-element.7) | data formatting | bytes 16777216
  421.1 11.9 %copy.27 = bf16[64,256,1,1,256]{4,1,0,3,2:T(8,128)(2,1)S(1)} copy(bf16[64,256,1,1,256]{4,3,1,0,2:T(2,128)(2,1)} %get-tuple-element.8) | data formatting | bytes 16777216
  433.1 3.2 copy-done.1
  436.3 3.3 fusion.21
  439.6 9.5 %fusion.17 = f32[64,128,256]{2,1,0:T(8,128)} fusion(bf16[64,256,256]{2,1,0:T(8,128)(2,1)} %bitcast.62, bf16[64,256,256]{2,1,0:T(8,128)(2,1)S(1)} %bitcast.58), kind=kOutput, calls=%fused_computation.29 | convolution fusion | flops 1073741824 | bytes 20971520 | tf_op jit(solution)/shard_map/cik,cjk->cij/dot_general | solution.py:57
  449.0 6.8 fusion.37
  455.9 10.1 %fusion.13 = f32[64,128,128]{2,1,0:T(8,128)} fusion(bf16[64,256,512]{2,1,0:T(8,128)(2,1)} %bitcast.55), kind=kOutput, calls=%fused_computation.21 | convolution fusion | flops 1073741824 | bytes 12582912 | tf_op jit(solution)/shard_map/cik,cjk->cij/dot_general | solution.py:45
  466.0 15.0 %pad_select_fusion = f32[64,128,256]{2,1,0:T(8,128)} fusion(f32[64,128,128]{2,1,0:T(8,128)} %fusion.37, pred[128,256]{1,0:T(8,128)(4,1)S(1)} %iota_compare_fusion.1, bf16[64,256,512]{2,1,0:T(8,128)(2,1)} %bitcast.56), kind=kOutput, calls=%fused_computation.28 | convolution fusion | flops 2149580800 | bytes 37781504 | tf_op jit(solution)/shard_map/cik,cjk->cij/dot_general | solution.py:45
  481.0 14.2 %subtract_select_fusion = f32[64,128,256]{2,1,0:T(8,128)} fusion(f32[64,128,256]{2,1,0:T(8,128)} %fusion.17, f32[64,128,128]{2,1,0:T(8,128)} %fusion.13, pred[128,256]{1,0:T(8,128)(4,1)S(1)} %iota_compare_fusion, bf16[64,256,256]{2,1,0:T(8,128)(2,1)} %bitcast.60, bf16[64,256,256]{2,1,0:T(8,128)(2,1)} %bitcast.64), kind=kOutput, calls=%fused_computation.27 | convolution fusion | flops 1077936128 | bytes 33587200 | tf_op jit(solution)/shard_map/cik,cjk->cij/dot_general | solution.py:51
  495.2 11.4 %maximum_multiply_fusion = f32[64,256,256]{2,1,0:T(8,128)} fusion(f32[64,128,256]{2,1,0:T(8,128)} %subtract_select_fusion, f32[64,128,256]{2,1,0:T(8,128)} %pad_select_fusion), kind=kLoop, calls=%fused_computation.12 | loop fusion | flops 8388608 | bytes 33554432 | tf_op jit(solution)/shard_map/div | solution.py:67
  506.7 0.0 reduce-scatter.2.cloned.1.call-update
  506.7 0.6 copy-done.4
  507.3 0.1 dynamic-slice_convert_fusion
  507.4 278.1 %reduce-scatter.2.cloned.1.call-done = f32[16,256,256]{2,1,0:T(8,128)} async-done(((f32[64,256,256]{2,1,0:T(8,128)}), f32[16,256,256]{2,1,0:T(8,128)}) %reduce-scatter.2.cloned.1.call-update) | async-done | bytes 4194320 | tf_op jit(solution)/shard_map/reduce_scatter | solution.py:100
  785.5 4.7 broadcast_multiply_fusion
  (13 shorter events, 0.1 us)
Async XLA Ops:
  6.5 29.0 %copy-start.3 = (f32[32]{0:T(128)S(1)}, f32[32]{0:T(128)}, u32[]{:S(2)}) copy-start(f32[32]{0:T(128)} %param.6) | copy-start | bytes 388
  6.5 29.3 %copy-start.2 = (f32[4,1024]{1,0:T(4,128)S(1)}, f32[4,1024]{1,0:T(4,128)}, u32[]{:S(2)}) copy-start(f32[4,1024]{1,0:T(4,128)} %param.5) | copy-start | bytes 49156
  22.1 13.8 %collective-permute-start = (bf16[32,3,1024]{2,1,0:T(4,128)(2,1)S(1)}, bf16[32,3,1024]{2,1,0:T(4,128)(2,1)S(1)}, u32[]{:S(2)}, u32[]{:S(2)}) collective-permute-start(bf16[32,3,1024]{2,1,0:T(4,128)(2,1)S(1)} %slice.79), channel_id=1, source_target_pairs={{0,1},{1,2},{2,3},{4,5},{5,6},{6,7},{8,9},{9,10},{10,11},{12,13},{... | collective-permute-start | bytes 589832 | tf_op jit(solution)/shard_map/ppermute | solution.py:11
  152.3 189.7 %all-to-all-start = ((bf16[512,32,512]{2,1,0:T(8,128)(2,1)}), bf16[512,32,512]{2,1,0:T(8,128)(2,1)}, u32[]{:S(2)}, u32[]{:S(2)}) async-start(bf16[512,32,512]{2,1,0:T(8,128)(2,1)} %copy.14), calls=%async_computation | async-start | bytes 33554432 | tf_op jit(solution)/shard_map/all_to_all | solution.py:99
  158.0 627.5 %reduce-scatter.2.cloned.1.call-start = ((), (), s32[]{:S(2)}) async-start(), calls=%async_computation.2 | async-start | bytes 20971520 | tf_op jit(solution)/shard_map/reduce_scatter | solution.py:100
  421.1 28.0 %copy-start = (bf16[64,256,1,1,256]{4,1,0,3,2:T(8,128)(2,1)}, bf16[64,256,1,1,256]{4,1,0,3,2:T(8,128)(2,1)S(1)}, u32[]{:S(2)}) copy-start(bf16[64,256,1,1,256]{4,1,0,3,2:T(8,128)(2,1)S(1)} %copy.26) | copy-start | bytes 25165828
  433.1 3.2 copy-start.1
  506.7 0.7 copy-start.4
Sparse Core Ops, SparseCore 0:
  506.8 278.6 reduce-scatter.1
where the time goes:
time: 799 us; the launch traced here: 797 us
  waiting for transfers between devices  462 us (58%)
  local copies, waits for them, and re-layouts  139 us (17%)
  matrix products  116 us (15%)
  other arithmetic  55.9 us (7%)
  between operations  13.6 us (2%)
  starting transfers between devices  10.9 us (1%)
    reduce_scatter x1, waiting for transfers between devices, on_device(): lax.psum_scatter(gram_blocks(turned, local_frame_count, frame_total), 'tm...  278 us
    all_to_all x1, waiting for transfers between devices, on_device(): lax.all_to_all(spectra, 'feed', split_axis=0, concat_axis=1, tiled=True)  184 us
    dot_general x1, matrix products, on_device(): jnp.einsum('cpn,isn->cips', dft_table, filtered, preferred_element_type=j...  56.9 us
    unnamed x13, local copies, waits for them, and re-layouts  40.1 us
    slice x1, local copies, waits for them, and re-layouts, gram_blocks(): real_half = split[:, :, :, 0].reshape(count_here, inputs_all, columns // 2)  32.4 us
    concatenate x1, local copies, waits for them, and re-layouts, on_device(): jnp.concatenate([real_part, imag_part], axis=2).astype(jnp.bfloat16)  28.6 us
    dot_general x2, matrix products, gram_blocks(): jnp.einsum('cik,cjk->cij', turned[:, first:last], turned[:, first:], pref...  25.1 us
    reshape x1, local copies, waits for them, and re-layouts, gram_blocks(): turned.reshape(count_here, inputs_all, columns // (2 * local_frame_count)...  23.7 us
  transfers between devices with their start and end apart: 3, of which 2 were waited for; matrix products, arithmetic and copies ran while one was open for 1% of the time, Pallas kernels for 0%

commit v1 on v0

--- a/solution.py
+++ b/solution.py
@@ -96,7 +96,10 @@
     local_flags = lax.dynamic_slice_in_dim(
         channel_flags, lax.axis_index("tm") * channels_here, channels_here, 0
     )
-    turned = lax.all_to_all(spectra, "feed", split_axis=0, concat_axis=1, tiled=True)
+    turned = jnp.concatenate(
+        lax.all_to_all(jnp.stack(jnp.split(spectra, lax.axis_size("feed"), axis=0)), "feed", 0, 0),
+        axis=1,
+    )
     visibility = lax.psum_scatter(
         gram_blocks(turned, local_frame_count, frame_total), "tm", scatter_dimension=0, tiled=True
     )

time: 799 us -> 823 us (1.030)
  other arithmetic: 55.9 us -> 71.6 us
    another operation x0 -> x2, local copies, waits for them, and re-layouts: none -> 60.2 us  [the longest x1 36.5 us: on_device(): jnp.stack(jnp.split(spectra, lax.axis_size('feed'), axis=0))]
    concatenate x1 -> x0, local copies, waits for them, and re-layouts: 28.6 us -> none  [on_device(): jnp.concatenate([real_part, imag_part], axis=2).astype(jnp.bfloat16)]
    unnamed x0 -> x7, other arithmetic: none -> 19 us
    all_to_all x1 -> x0, local copies, waits for them, and re-layouts: 14.1 us -> none  [on_device(): lax.all_to_all(spectra, 'feed', split_axis=0, concat_axis=1, tiled=True)]
    reshape x1, local copies, waits for them, and re-layouts: 23.7 us -> 14.1 us  [on_device(): jnp.concatenate(lax.all_to_all(jnp.stack(jnp.split(spectra, lax.axis_size...]
    another operation x2 -> x3, other arithmetic: 20.8 us -> 24 us
where the time goes in v1:
time: 823 us; the launch traced here: 821 us
  waiting for transfers between devices  462 us (56%)
  local copies, waits for them, and re-layouts  147 us (18%)
  matrix products  116 us (14%)
  other arithmetic  71.6 us (9%)
  between operations  13.6 us (2%)
  starting transfers between devices  10.7 us (1%)
    reduce_scatter x1, waiting for transfers between devices, on_device(): lax.psum_scatter(gram_blocks(turned, local_frame_count, frame_total), 'tm...  278 us
    all_to_all x1, waiting for transfers between devices, on_device(): lax.all_to_all(jnp.stack(jnp.split(spectra, lax.axis_size('feed'), axis=0...  184 us
    dot_general x1, matrix products, on_device(): jnp.einsum('cpn,isn->cips', dft_table, filtered, preferred_element_type=j...  56.9 us
    unnamed x13, local copies, waits for them, and re-layouts  40.1 us
    another operation x1, local copies, waits for them, and re-layouts, on_device(): jnp.stack(jnp.split(spectra, lax.axis_size('feed'), axis=0))  36.5 us
    slice x1, local copies, waits for them, and re-layouts, gram_blocks(): real_half = split[:, :, :, 0].reshape(count_here, inputs_all, columns // 2)  32.4 us
    dot_general x2, matrix products, gram_blocks(): jnp.einsum('cik,cjk->cij', turned[:, first:last], turned[:, first:], pref...  25.1 us
    another operation x1, local copies, waits for them, and re-layouts, gram_blocks(): turned.reshape(count_here, inputs_all, columns // (2 * local_frame_count)...  23.7 us
  transfers between devices with their start and end apart: 3, of which 2 were waited for; matrix products, arithmetic and copies ran while one was open for 1% of the time, Pallas kernels for 0%

profile of v1, /device:TPU:0, one launch (start us, length us, event | category | flops | bytes accessed | tf_op | source)
XLA Modules:
  0.0 820.6 jit_solution(9698383115097426338)
XLA Ops:
  6.5 15.4 %copy.24 = bf16[4,8,256,1024]{3,2,1,0:T(8,128)(2,1)S(1)} copy(bf16[4,8,256,1024]{3,1,2,0:T(8,128)(2,1)} %bitcast.97) | data formatting | bytes 33554432
  22.1 4.9 collective-permute-start
  27.0 8.5 %negate_convert_fusion = (bf16[512,1,1024]{2,0,1:T(8,128)(2,1)S(1)}, bf16[512,1,1024]{2,0,1:T(8,128)(2,1)S(1)}) fusion(), kind=kLoop, calls=%fused_computation.86 | loop fusion | flops 8912896 | bytes 2097152 | tf_op jit(solution)/shard_map/convert.3
  35.9 12.0 %maximum_convert_fusion = f32[32,259,1024]{2,1,0:T(8,128)} fusion(bf16[32,256,1024]{2,1,0:T(8,128)(2,1)S(1)} %bitcast.96, bf16[32,3,1024]{2,1,0:T(4,128)(2,1)S(1)} %collective-permute-done), kind=kLoop, calls=%fused_computation.22 | loop fusion | flops 33947648 | bytes 50921472 | tf_op jit(solution)/shard_map/convert_element_type | solution.py:76
  47.9 56.9 %fusion.10 = f32[512,32,2,256]{0,3,2,1:T(8,128)} fusion(f32[32,259,1024]{2,1,0:T(8,128)} %maximum_convert_fusion, f32[1024]{0:T(1024)S(1)} %bitcast.100, f32[1024]{0:T(1024)S(1)} %bitcast.101, f32[1024]{0:T(1024)S(1)} %bitcast.99, f32[1024]{0:T(1024)S(1)} %bitcast.98, bf16[512,1,1024]{2,0,1:T(8,128)(2,1)S(1)} %get-tuple-element.15, ...), kind=kOutput, calls=%fused_computation.33 | convolution fusion | flops 17251172352 | bytes 169885696 | tf_op jit(solution)/shard_map/cpn,isn->cips/dot_general | solution.py:85
  104.8 12.3 %multiply_convert_fusion = (bf16[512,32,256]{0,2,1:T(8,128)(2,1)S(1)}, bf16[512,32,256]{0,2,1:T(8,128)(2,1)S(1)}) fusion(f32[512,32,2,256]{0,3,2,1:T(8,128)} %fusion.10, f32[512,32]{0,1:T(8,128)S(1)} %get-tuple-element.14, f32[512,32]{0,1:T(8,128)S(1)} %get-tuple-element.13), kind=kLoop, calls=%fused_computation.28 | loop fusion | flops 41943040 | bytes 50462720 | tf_op jit(solution)/shard_map/convert.1
  117.1 2.4 fusion.22
  119.5 3.2 fusion.25
  122.7 2.4 fusion.28
  125.0 3.2 fusion.31
  128.2 2.3 fusion.34
  130.5 3.2 fusion.37
  133.7 2.4 fusion.19
  136.1 3.2 fusion.43
  139.3 36.5 %copy.15 = bf16[8,64,32,512]{3,2,1,0:T(8,128)(2,1)} copy(bf16[8,64,32,512]{1,3,2,0:T(8,128)(2,1)} %fusion.43) | data formatting | bytes 33554432 | tf_op jit(solution)/shard_map/stack | solution.py:100
  175.8 5.7 all-to-all-start
  181.7 183.8 %all-to-all-done = bf16[8,64,32,512]{3,2,1,0:T(8,128)(2,1)} async-done(((bf16[8,64,32,512]{3,2,1,0:T(8,128)(2,1)}), bf16[8,64,32,512]{3,2,1,0:T(8,128)(2,1)}, u32[]{:S(2)}, u32[]{:S(2)}) %all-to-all-start) | async-done | bytes 16777248 | tf_op jit(solution)/shard_map/all_to_all | solution.py:100
  365.5 14.1 %copy.16 = bf16[64,8,32,512]{3,2,1,0:T(8,128)(2,1)} copy(bf16[64,8,32,512]{3,2,0,1:T(8,128)(2,1)} %bitcast.18) | data formatting | bytes 33554432 | tf_op jit(solution)/shard_map/reshape | solution.py:99
  379.6 23.7 %reshape_reshape.3 = bf16[64,256,1,2,256]{4,3,1,0,2:T(2,128)(2,1)} reshape(bf16[64,8,32,512]{3,2,1,0:T(8,128)(2,1)} %copy.16) | data formatting | bytes 33554432 | tf_op jit(solution)/shard_map/reshape;reshape | solution.py:35
  403.3 32.4 %fusion.68 = (bf16[64,256,1,1,256]{4,3,1,0,2:T(2,128)(2,1)}, bf16[64,256,1,1,256]{4,3,1,0,2:T(2,128)(2,1)}) fusion(bf16[64,256,1,2,256]{4,3,1,0,2:T(2,128)(2,1)} %reshape_reshape.3), kind=kLoop, calls=%fused_computation.100 | loop fusion | bytes 33554432 | tf_op jit(solution)/shard_map/slice | solution.py:38
  435.7 8.9 %copy.27 = bf16[64,256,1,1,256]{4,1,0,3,2:T(8,128)(2,1)S(1)} copy(bf16[64,256,1,1,256]{4,3,1,0,2:T(2,128)(2,1)} %get-tuple-element.7) | data formatting | bytes 16777216
  444.6 11.9 %copy.28 = bf16[64,256,1,1,256]{4,1,0,3,2:T(8,128)(2,1)S(1)} copy(bf16[64,256,1,1,256]{4,3,1,0,2:T(2,128)(2,1)} %get-tuple-element.8) | data formatting | bytes 16777216
  456.6 3.2 copy-done.1
  459.8 3.3 fusion.44
  463.1 9.5 %fusion.38 = f32[64,128,256]{2,1,0:T(8,128)} fusion(bf16[64,256,256]{2,1,0:T(8,128)(2,1)} %bitcast.92, bf16[64,256,256]{2,1,0:T(8,128)(2,1)S(1)} %bitcast.88), kind=kOutput, calls=%fused_computation.63 | convolution fusion | flops 1073741824 | bytes 20971520 | tf_op jit(solution)/shard_map/cik,cjk->cij/dot_general | solution.py:57
  472.6 6.8 fusion.60
  479.4 10.1 %fusion.13 = f32[64,128,128]{2,1,0:T(8,128)} fusion(bf16[64,256,512]{2,1,0:T(8,128)(2,1)} %bitcast.85), kind=kOutput, calls=%fused_computation.34 | convolution fusion | flops 1073741824 | bytes 12582912 | tf_op jit(solution)/shard_map/cik,cjk->cij/dot_general | solution.py:45
  489.5 15.0 %pad_select_fusion = f32[64,128,256]{2,1,0:T(8,128)} fusion(f32[64,128,128]{2,1,0:T(8,128)} %fusion.60, pred[128,256]{1,0:T(8,128)(4,1)S(1)} %iota_compare_fusion.1, bf16[64,256,512]{2,1,0:T(8,128)(2,1)} %bitcast.86), kind=kOutput, calls=%fused_computation.41 | convolution fusion | flops 2149580800 | bytes 37781504 | tf_op jit(solution)/shard_map/cik,cjk->cij/dot_general | solution.py:45
  504.6 14.2 %subtract_select_fusion = f32[64,128,256]{2,1,0:T(8,128)} fusion(f32[64,128,256]{2,1,0:T(8,128)} %fusion.38, f32[64,128,128]{2,1,0:T(8,128)} %fusion.13, pred[128,256]{1,0:T(8,128)(4,1)S(1)} %iota_compare_fusion, bf16[64,256,256]{2,1,0:T(8,128)(2,1)} %bitcast.90, bf16[64,256,256]{2,1,0:T(8,128)(2,1)} %bitcast.94), kind=kOutput, calls=%fused_computation.40 | convolution fusion | flops 1077936128 | bytes 33587200 | tf_op jit(solution)/shard_map/cik,cjk->cij/dot_general | solution.py:51
  518.8 11.4 %maximum_multiply_fusion = f32[64,256,256]{2,1,0:T(8,128)} fusion(f32[64,128,256]{2,1,0:T(8,128)} %subtract_select_fusion, f32[64,128,256]{2,1,0:T(8,128)} %pad_select_fusion), kind=kLoop, calls=%fused_computation.25 | loop fusion | flops 8388608 | bytes 33554432 | tf_op jit(solution)/shard_map/div | solution.py:67
  530.9 278.1 %reduce-scatter.2.cloned.1.call-done = f32[16,256,256]{2,1,0:T(8,128)} async-done(((f32[64,256,256]{2,1,0:T(8,128)}), f32[16,256,256]{2,1,0:T(8,128)}) %reduce-scatter.2.cloned.1.call-update) | async-done | bytes 4194320 | tf_op jit(solution)/shard_map/reduce_scatter | solution.py:103
  809.0 4.7 broadcast_multiply_fusion
  (20 shorter events, 1.3 us)
Async XLA Ops:
  6.5 29.0 %copy-start.3 = (f32[32]{0:T(128)S(1)}, f32[32]{0:T(128)}, u32[]{:S(2)}) copy-start(f32[32]{0:T(128)} %param.6) | copy-start | bytes 388
  6.5 29.3 %copy-start.2 = (f32[4,1024]{1,0:T(4,128)S(1)}, f32[4,1024]{1,0:T(4,128)}, u32[]{:S(2)}) copy-start(f32[4,1024]{1,0:T(4,128)} %param.5) | copy-start | bytes 49156
  22.1 13.8 %collective-permute-start = (bf16[32,3,1024]{2,1,0:T(4,128)(2,1)S(1)}, bf16[32,3,1024]{2,1,0:T(4,128)(2,1)S(1)}, u32[]{:S(2)}, u32[]{:S(2)}) collective-permute-start(bf16[32,3,1024]{2,1,0:T(4,128)(2,1)S(1)} %slice.79), channel_id=1, source_target_pairs={{0,1},{1,2},{2,3},{4,5},{5,6},{6,7},{8,9},{9,10},{10,11},{12,13},{... | collective-permute-start | bytes 589832 | tf_op jit(solution)/shard_map/ppermute | solution.py:11
  175.8 189.7 %all-to-all-start = ((bf16[8,64,32,512]{3,2,1,0:T(8,128)(2,1)}), bf16[8,64,32,512]{3,2,1,0:T(8,128)(2,1)}, u32[]{:S(2)}, u32[]{:S(2)}) async-start(bf16[8,64,32,512]{3,2,1,0:T(8,128)(2,1)} %copy.15), calls=%async_computation | async-start | bytes 33554432 | tf_op jit(solution)/shard_map/all_to_all | solution.py:100
  181.5 627.5 %reduce-scatter.2.cloned.1.call-start = ((), (), s32[]{:S(2)}) async-start(), calls=%async_computation.2 | async-start | bytes 20971520 | tf_op jit(solution)/shard_map/reduce_scatter | solution.py:103
  444.6 28.0 %copy-start = (bf16[64,256,1,1,256]{4,1,0,3,2:T(8,128)(2,1)}, bf16[64,256,1,1,256]{4,1,0,3,2:T(8,128)(2,1)S(1)}, u32[]{:S(2)}) copy-start(bf16[64,256,1,1,256]{4,1,0,3,2:T(8,128)(2,1)S(1)} %copy.27) | copy-start | bytes 25165828
  456.6 3.2 copy-start.1
  530.2 0.7 copy-start.4
Sparse Core Ops, SparseCore 0:
  530.4 278.6 reduce-scatter.1
